TPU v7x, 256 devices: a whole 4x4x8 slice. The times are simulated.
256 devices in a mesh: ctx: 64 (over y, z, core), head: 4 (over x).
Axes of the slice: x: 4, y: 4, z: 8, core: 2. Of those that a mesh axis runs over, the one named last changes fastest.
Arguments:
- q_lin: bfloat16 [8192, 8192], P('ctx', 'head'), may hold values from -6 to 6
- k_lin: bfloat16 [8192, 8192], P('ctx', 'head'), may hold values from -6 to 6
- v_lin: bfloat16 [8192, 8192], P('ctx', 'head'), may hold values from -70 to 70
- log_decay: float32 [64, 8192], P('head', 'ctx'), may hold values from -1 to 0
- gate: bfloat16 [8192, 8192], P('ctx', 'head'), may hold values from -6 to 6
- norm_gain: float32 [8192], P('head'), may hold values from 0.1 to 1.9
- queries: bfloat16 [8192, 8192], P('ctx', 'head'), may hold values from -8 to 8
- keys: bfloat16 [8192, 1024], P('ctx', 'head'), may hold values from -4 to 4
- values: bfloat16 [8192, 1024], P('ctx', 'head'), may hold values from -6 to 6
- order: int32 [64], P('ctx'), may hold values from 0 to 63, each once
Outputs:
- mixed: bfloat16 [8192, 8192], P('ctx', 'head')
- attended: bfloat16 [8192, 8192], P('ctx', 'head')
Inputs may be any that keep to these rules, and one draw needn't show every extreme that they name: order is a permutation of the 64 sequence shards.
All inputs are finite; a program needn't handle non-finite values.
Results may differ from a plain program's by a relative error of at most 0.0045.
Values may be sent and summed in bfloat16 or wider, within the bound.
A program may use at most 128 MiB of HBM per device.

v0:
```python
import math

import jax
import jax.numpy as jnp
from jax import lax
from jax.sharding import Mesh
from jax.sharding import PartitionSpec as P

H = 64
HD = 128
BLOCK = 128
CTX = ("ctx_0", "ctx_1", "ctx_2")


EPS = 1e-06


def nothing_yet(array, identity):
    return jax.tree.map(
        lambda a, e: jnp.broadcast_to(jnp.asarray(e, a.dtype), a.shape), array, identity
    )


def carried_in(array, axes, combine, identity):
    before = start = nothing_yet(array, identity)
    subtotal = array
    for axis in reversed(axes):
        size, index = (lax.axis_size(axis), lax.axis_index(axis))
        pieces = jax.tree.map(lambda part: lax.all_gather(part, axis), subtotal)
        inside, subtotal = (start, start)
        for k in range(size):
            passed = k < index
            subtotal = combine(subtotal, jax.tree.map(lambda part: part[k], pieces))
            inside = jax.tree.map(lambda new, old: jnp.where(passed, new, old), subtotal, inside)
        before = combine(inside, before)
    return before


def sent_to_all(array, axis):
    size = lax.axis_size(axis)
    return lax.all_to_all(
        jnp.broadcast_to(array[None], (size, *array.shape)), axis, 0, 0, tiled=True
    )


def over_copies(array, axis):
    return sent_to_all(array, axis).sum(axis=0)


def in_one_piece(arrays, axis, dim, along):
    widths = [a.shape[along] for a in arrays]
    both = jnp.concatenate(arrays, axis=along)
    whole = lax.all_gather(both, axis, axis=dim, tiled=True)
    return tuple(jnp.split(whole, [sum(widths[:k]) for k in range(1, len(widths))], axis=along))


def lightning_blocks(qa, ka, va, decay_log, state0):
    total = qa.shape[0]
    heads = qa.shape[1]
    count = total // BLOCK
    qb_all = qa.reshape(count, BLOCK, heads, HD)
    kb_all = ka.reshape(count, BLOCK, heads, HD)
    vb_all = va.reshape(count, BLOCK, heads, HD)
    gb_all = decay_log.reshape(heads, count, BLOCK).transpose(1, 0, 2)

    def step(state, pieces):
        qb, kb, vb, gb = pieces
        cum = jnp.cumsum(gb, axis=1)
        scores = jnp.einsum("thd,shd->hts", qb, kb, preferred_element_type=jnp.float32)
        lower = lax.iota(jnp.int32, BLOCK)[:, None] >= lax.iota(jnp.int32, BLOCK)[None, :]
        diff = cum[:, :, None] - cum[:, None, :]
        decay = jnp.where(lower[None], jnp.exp(jnp.where(lower[None], diff, 0.0)), 0.0)
        weights = (scores * decay).astype(jnp.bfloat16)
        intra = jnp.einsum("hts,shd->thd", weights, vb, preferred_element_type=jnp.float32)
        qdec = qb.astype(jnp.float32) * jnp.exp(cum).T[:, :, None]
        inter = jnp.einsum("thd,hde->the", qdec, state)
        kdec = kb.astype(jnp.float32) * jnp.exp(cum[:, -1:] - cum).T[:, :, None]
        update = jnp.einsum("thd,the->hde", kdec, vb.astype(jnp.float32))
        state_new = jnp.exp(cum[:, -1])[:, None, None] * state + update
        return (state_new, intra + inter)

    state, outs = lax.scan(step, state0, (qb_all, kb_all, vb_all, gb_all))
    return (outs.reshape(total, heads, HD), state)


def combine_states(earlier, later):
    return (earlier[0] * later[0], later[0][:, None, None] * earlier[1] + later[1])


def body(q_lin, k_lin, v_lin, log_decay, gate, norm_gain, queries, keys, values, order):
    tokens = q_lin.shape[0]
    heads = log_decay.shape[0]
    width = q_lin.shape[1]
    qa = jax.nn.silu(q_lin.astype(jnp.float32)).astype(jnp.bfloat16).reshape(tokens, heads, HD)
    ka = jax.nn.silu(k_lin.astype(jnp.float32)).astype(jnp.bfloat16).reshape(tokens, heads, HD)
    va = jax.nn.silu(v_lin.astype(jnp.float32)).astype(jnp.bfloat16).reshape(tokens, heads, HD)
    empty = jnp.zeros((heads, HD, HD), jnp.float32)
    decay_total = jnp.exp(jnp.sum(log_decay, axis=1))
    unit = jnp.ones_like(decay_total)
    local_out, local_state = lightning_blocks(qa, ka, va, log_decay, empty)
    prefix = carried_in((decay_total, local_state), CTX, combine_states, (unit, empty))
    carried = prefix[1]
    cum_full = jnp.cumsum(log_decay, axis=1)
    qdec = qa.astype(jnp.float32) * jnp.exp(cum_full).T[:, :, None]
    lin = local_out + jnp.einsum("thd,hde->the", qdec, carried)
    squares = jnp.sum(lin * lin, axis=(1, 2))
    total = over_copies(squares, "head")
    inv = lax.rsqrt(total / (H * HD) + EPS)
    gated = jax.nn.sigmoid(gate.astype(jnp.float32).reshape(tokens, heads, HD))
    mixed = (
        (lin * inv[:, None, None] * norm_gain.reshape(heads, HD) * gated)
        .astype(jnp.bfloat16)
        .reshape(tokens, width)
    )
    kv_heads = keys.shape[1] // HD
    group = heads // kv_heads
    qgroup = queries.reshape(tokens, kv_heads, group, HD)
    first_pos = order[0] * tokens
    qpos = first_pos + lax.iota(jnp.int32, tokens)
    last_pos = first_pos + tokens - 1
    scale = 1.0 / math.sqrt(HD)

    def update(carry, kblock, vblock, kstart):
        top, den, acc = carry
        count = kblock.shape[0]
        kparts = kblock.reshape(count, kv_heads, HD)
        vparts = vblock.reshape(count, kv_heads, HD)
        scores = (
            jnp.einsum("tkgd,skd->kgts", qgroup, kparts, preferred_element_type=jnp.float32) * scale
        )
        kpos = kstart + lax.iota(jnp.int32, count)
        mask = kpos[None, :] <= qpos[:, None]
        masked = jnp.where(mask, scores, -1e30)
        top_new = jnp.maximum(top, jnp.max(masked, axis=-1))
        alpha = jnp.exp(top - top_new)
        probs = jnp.where(mask, jnp.exp(masked - top_new[..., None]), 0.0)
        den_new = den * alpha + jnp.sum(probs, axis=-1)
        acc_new = acc * alpha[..., None] + jnp.einsum(
            "kgts,skd->kgtd", probs.astype(jnp.bfloat16), vparts, preferred_element_type=jnp.float32
        )
        return (top_new, den_new, acc_new)

    def visit(carry, kblock, vblock, kstart):
        return lax.cond(
            kstart > last_pos,
            lambda held: held,
            lambda held: update(held, kblock, vblock, kstart),
            carry,
        )

    init = (
        jnp.full((kv_heads, group, tokens), -1e30, jnp.float32),
        jnp.zeros((kv_heads, group, tokens), jnp.float32),
        jnp.zeros((kv_heads, group, tokens, HD), jnp.float32),
    )
    kpiece, vpiece = in_one_piece((keys, values), CTX, 0, 1)
    rows = kpiece.shape[0]
    stride = 512
    count = rows // stride

    def loop_body(index, held):
        offset = index * stride
        kslice = lax.dynamic_slice_in_dim(kpiece, offset, stride, 0)
        vslice = lax.dynamic_slice_in_dim(vpiece, offset, stride, 0)
        return visit(held, kslice, vslice, offset)

    top, den, acc = lax.fori_loop(0, count, loop_body, init)
    attended = (
        (acc / den[..., None]).transpose(2, 0, 1, 3).reshape(tokens, width).astype(jnp.bfloat16)
    )
    return (mixed, attended)


def solution(mesh):
    finer = Mesh(
        mesh.devices.reshape(4, 8, 2, mesh.shape["head"]), ("ctx_0", "ctx_1", "ctx_2", "head")
    )
    in_specs = (
        P(CTX, "head"),
        P(CTX, "head"),
        P(CTX, "head"),
        P("head", CTX),
        P(CTX, "head"),
        P("head"),
        P(CTX, "head"),
        P(CTX, "head"),
        P(CTX, "head"),
        P(CTX),
    )
    out_specs = (P(CTX, "head"), P(CTX, "head"))
    return jax.shard_map(body, mesh=finer, in_specs=in_specs, out_specs=out_specs, check_vma=False)
```

profile of v0, /device:TPU:32, one launch (start us, length us, event | category | flops | bytes accessed | tf_op | source)
XLA Modules:
  0.0 329.3 jit_solution(18312880730397345031)
XLA Ops:
  18.2 13.4 %all-gather.15.cloned.1.call-done = f32[32,128,128]{2,1,0:T(8,128)} async-done(((f32[16,128,128]{2,1,0:T(8,128)}), f32[32,128,128]{2,1,0:T(8,128)}) %all-gather.15.cloned.1.call-update) | async-done | bytes 2097168 | tf_op jit(solution)/shard_map/all_gather | solution.py:29
  35.4 16.3 %all-reduce.1 = f32[128]{0:T(128)S(1)} all-reduce(f32[128]{0:T(128)S(1)} %get-tuple-element.408), channel_id=4, replica_groups=mesh['ctx_0'=4,'ctx_1'=8,'ctx_2'=2,'head'=4] {'ctx_1'}, use_global_device_ids=true, to_apply=%add.1 | all-reduce | flops 128 | bytes 1024
  51.8 76.3 %all-gather.9.cloned.1.call-done = f32[8,16,128,128]{3,2,1,0:T(8,128)} async-done(((f32[1,16,128,128]{3,2,1,0:T(8,128)}), f32[8,16,128,128]{3,2,1,0:T(8,128)}) %all-gather.9.cloned.1.call-update) | async-done | bytes 8388624 | tf_op jit(solution)/shard_map/all_gather | solution.py:29
  128.1 5.1 %multiply_add_fusion.1 = f32[1,16,128,128]{3,2,1,0:T(8,128)} fusion(f32[8,16,128,128]{3,2,1,0:T(8,128)} %all-gather.9.cloned.1.call-done, f32[16]{0:T(128)S(1)} %get-tuple-element.401, f32[16]{0:T(128)S(1)} %get-tuple-element.406, f32[16]{0:T(128)S(1)} %get-tuple-element.405, f32[16]{0:T(128)S(1)} %get-tuple-element.404, f32[16]{0:T(128)S(1)} %get-tuple-element.403, ...), kind=kLoop, calls=%fused_computation.98 | loop fusion | flops 3932160 | bytes 9437696 | tf_op jit(solution)/shard_map/add | solution.py:87
  135.2 9.9 %all-gather.3 = f32[4,1,16]{2,1,0:T(1,128)S(1)} all-gather(f32[1,1,16]{2,1,0:T(1,128)S(1)} %fusion.142), channel_id=1, replica_groups=mesh['ctx_0'=4,'ctx_1'=8,'ctx_2'=2,'head'=4] {'ctx_0'}, dimensions={0}, use_global_device_ids=true | all-gather | bytes 320 | tf_op jit(solution)/shard_map/all_gather | solution.py:29
  151.4 65.3 %all-gather.13.cloned.1.call-done = bf16[8192,512]{0,1:T(8,128)(2,1)} async-done(((bf16[128,512]{0,1:T(8,128)(2,1)}), bf16[8192,512]{0,1:T(8,128)(2,1)}) %all-gather.13.cloned.1.call-update) | async-done | bytes 8388624 | tf_op jit(solution)/shard_map/all_gather | solution.py:53
  216.8 6.0 %fusion.147 = (bf16[8192,256]{0,1:T(8,128)(2,1)}, bf16[8192,256]{0,1:T(8,128)(2,1)}) fusion(bf16[8192,512]{0,1:T(8,128)(2,1)} %all-gather.13.cloned.1.call-done), kind=kLoop, calls=%fused_computation.204 | loop fusion | bytes 16777216 | tf_op jit(solution)/shard_map/split | solution.py:54
  222.9 78.4 %while.5 = (s32[]{:T(128)}, f32[2,8,128]{2,1,0:T(8,128)S(1)}, f32[2,8,128]{2,1,0:T(8,128)S(1)}, f32[2,8,128,128]{3,2,1,0:T(8,128)S(1)}, s32[]{:T(128)}, /*index=...) while((s32[]{:T(128)}, f32[2,8,128]{2,1,0:T(8,128)S(1)}, ...), condition=%wide.region_9.10_spmd.clone, body=%wide.region_4.9_spmd.clone.sunk | while | flops 551096960 | bytes 17176876 | solution.py:167
  222.9 4.8 %conditional.3 = (f32[2,8,128]{2,1,0:T(8,128)S(1)}, f32[2,8,128]{2,1,0:T(8,128)S(1)}, f32[2,8,128,128]{3,2,1,0:T(8,128)S(1)}) conditional(s32[]{:T(128)} %convert_element_type.167, (s32[]{:T(128)}, s32[]{:T(128)}, bf16[8192,256]{0,1:T(8,128)(2,1)}, bf16[128,2,8,128]{3,0,2,1:T(8,128)(2,1)S(1)}, f32[2,8,128]{2,1,0:T(8,128)S(1)}, ...), branch_computations={%region_5.7_spmd, %region_8.8_spmd} | conditional | flops 551096960 | bytes 17159750 | solution.py:144
  227.8 4.8 %conditional.3 = (f32[2,8,128]{2,1,0:T(8,128)S(1)}, f32[2,8,128]{2,1,0:T(8,128)S(1)}, f32[2,8,128,128]{3,2,1,0:T(8,128)S(1)}) conditional(s32[]{:T(128)} %convert_element_type.167, (s32[]{:T(128)}, s32[]{:T(128)}, bf16[8192,256]{0,1:T(8,128)(2,1)}, bf16[128,2,8,128]{3,0,2,1:T(8,128)(2,1)S(1)}, f32[2,8,128]{2,1,0:T(8,128)S(1)}, ...), branch_computations={%region_5.7_spmd, %region_8.8_spmd} | conditional | flops 551096960 | bytes 17159750 | solution.py:144
  232.7 4.9 %conditional.3 = (f32[2,8,128]{2,1,0:T(8,128)S(1)}, f32[2,8,128]{2,1,0:T(8,128)S(1)}, f32[2,8,128,128]{3,2,1,0:T(8,128)S(1)}) conditional(s32[]{:T(128)} %convert_element_type.167, (s32[]{:T(128)}, s32[]{:T(128)}, bf16[8192,256]{0,1:T(8,128)(2,1)}, bf16[128,2,8,128]{3,0,2,1:T(8,128)(2,1)S(1)}, f32[2,8,128]{2,1,0:T(8,128)S(1)}, ...), branch_computations={%region_5.7_spmd, %region_8.8_spmd} | conditional | flops 551096960 | bytes 17159750 | solution.py:144
  237.6 4.8 %conditional.3 = (f32[2,8,128]{2,1,0:T(8,128)S(1)}, f32[2,8,128]{2,1,0:T(8,128)S(1)}, f32[2,8,128,128]{3,2,1,0:T(8,128)S(1)}) conditional(s32[]{:T(128)} %convert_element_type.167, (s32[]{:T(128)}, s32[]{:T(128)}, bf16[8192,256]{0,1:T(8,128)(2,1)}, bf16[128,2,8,128]{3,0,2,1:T(8,128)(2,1)S(1)}, f32[2,8,128]{2,1,0:T(8,128)S(1)}, ...), branch_computations={%region_5.7_spmd, %region_8.8_spmd} | conditional | flops 551096960 | bytes 17159750 | solution.py:144
  242.5 4.9 %conditional.3 = (f32[2,8,128]{2,1,0:T(8,128)S(1)}, f32[2,8,128]{2,1,0:T(8,128)S(1)}, f32[2,8,128,128]{3,2,1,0:T(8,128)S(1)}) conditional(s32[]{:T(128)} %convert_element_type.167, (s32[]{:T(128)}, s32[]{:T(128)}, bf16[8192,256]{0,1:T(8,128)(2,1)}, bf16[128,2,8,128]{3,0,2,1:T(8,128)(2,1)S(1)}, f32[2,8,128]{2,1,0:T(8,128)S(1)}, ...), branch_computations={%region_5.7_spmd, %region_8.8_spmd} | conditional | flops 551096960 | bytes 17159750 | solution.py:144
  247.4 4.9 %conditional.3 = (f32[2,8,128]{2,1,0:T(8,128)S(1)}, f32[2,8,128]{2,1,0:T(8,128)S(1)}, f32[2,8,128,128]{3,2,1,0:T(8,128)S(1)}) conditional(s32[]{:T(128)} %convert_element_type.167, (s32[]{:T(128)}, s32[]{:T(128)}, bf16[8192,256]{0,1:T(8,128)(2,1)}, bf16[128,2,8,128]{3,0,2,1:T(8,128)(2,1)S(1)}, f32[2,8,128]{2,1,0:T(8,128)S(1)}, ...), branch_computations={%region_5.7_spmd, %region_8.8_spmd} | conditional | flops 551096960 | bytes 17159750 | solution.py:144
  252.3 4.8 %conditional.3 = (f32[2,8,128]{2,1,0:T(8,128)S(1)}, f32[2,8,128]{2,1,0:T(8,128)S(1)}, f32[2,8,128,128]{3,2,1,0:T(8,128)S(1)}) conditional(s32[]{:T(128)} %convert_element_type.167, (s32[]{:T(128)}, s32[]{:T(128)}, bf16[8192,256]{0,1:T(8,128)(2,1)}, bf16[128,2,8,128]{3,0,2,1:T(8,128)(2,1)S(1)}, f32[2,8,128]{2,1,0:T(8,128)S(1)}, ...), branch_computations={%region_5.7_spmd, %region_8.8_spmd} | conditional | flops 551096960 | bytes 17159750 | solution.py:144
  257.2 4.8 %conditional.3 = (f32[2,8,128]{2,1,0:T(8,128)S(1)}, f32[2,8,128]{2,1,0:T(8,128)S(1)}, f32[2,8,128,128]{3,2,1,0:T(8,128)S(1)}) conditional(s32[]{:T(128)} %convert_element_type.167, (s32[]{:T(128)}, s32[]{:T(128)}, bf16[8192,256]{0,1:T(8,128)(2,1)}, bf16[128,2,8,128]{3,0,2,1:T(8,128)(2,1)S(1)}, f32[2,8,128]{2,1,0:T(8,128)S(1)}, ...), branch_computations={%region_5.7_spmd, %region_8.8_spmd} | conditional | flops 551096960 | bytes 17159750 | solution.py:144
  262.1 4.8 %conditional.3 = (f32[2,8,128]{2,1,0:T(8,128)S(1)}, f32[2,8,128]{2,1,0:T(8,128)S(1)}, f32[2,8,128,128]{3,2,1,0:T(8,128)S(1)}) conditional(s32[]{:T(128)} %convert_element_type.167, (s32[]{:T(128)}, s32[]{:T(128)}, bf16[8192,256]{0,1:T(8,128)(2,1)}, bf16[128,2,8,128]{3,0,2,1:T(8,128)(2,1)S(1)}, f32[2,8,128]{2,1,0:T(8,128)S(1)}, ...), branch_computations={%region_5.7_spmd, %region_8.8_spmd} | conditional | flops 551096960 | bytes 17159750 | solution.py:144
  267.0 4.8 %conditional.3 = (f32[2,8,128]{2,1,0:T(8,128)S(1)}, f32[2,8,128]{2,1,0:T(8,128)S(1)}, f32[2,8,128,128]{3,2,1,0:T(8,128)S(1)}) conditional(s32[]{:T(128)} %convert_element_type.167, (s32[]{:T(128)}, s32[]{:T(128)}, bf16[8192,256]{0,1:T(8,128)(2,1)}, bf16[128,2,8,128]{3,0,2,1:T(8,128)(2,1)S(1)}, f32[2,8,128]{2,1,0:T(8,128)S(1)}, ...), branch_computations={%region_5.7_spmd, %region_8.8_spmd} | conditional | flops 551096960 | bytes 17159750 | solution.py:144
  271.9 4.8 %conditional.3 = (f32[2,8,128]{2,1,0:T(8,128)S(1)}, f32[2,8,128]{2,1,0:T(8,128)S(1)}, f32[2,8,128,128]{3,2,1,0:T(8,128)S(1)}) conditional(s32[]{:T(128)} %convert_element_type.167, (s32[]{:T(128)}, s32[]{:T(128)}, bf16[8192,256]{0,1:T(8,128)(2,1)}, bf16[128,2,8,128]{3,0,2,1:T(8,128)(2,1)S(1)}, f32[2,8,128]{2,1,0:T(8,128)S(1)}, ...), branch_computations={%region_5.7_spmd, %region_8.8_spmd} | conditional | flops 551096960 | bytes 17159750 | solution.py:144
  276.8 4.8 %conditional.3 = (f32[2,8,128]{2,1,0:T(8,128)S(1)}, f32[2,8,128]{2,1,0:T(8,128)S(1)}, f32[2,8,128,128]{3,2,1,0:T(8,128)S(1)}) conditional(s32[]{:T(128)} %convert_element_type.167, (s32[]{:T(128)}, s32[]{:T(128)}, bf16[8192,256]{0,1:T(8,128)(2,1)}, bf16[128,2,8,128]{3,0,2,1:T(8,128)(2,1)S(1)}, f32[2,8,128]{2,1,0:T(8,128)S(1)}, ...), branch_computations={%region_5.7_spmd, %region_8.8_spmd} | conditional | flops 551096960 | bytes 17159750 | solution.py:144
  286.6 4.8 %conditional.3 = (f32[2,8,128]{2,1,0:T(8,128)S(1)}, f32[2,8,128]{2,1,0:T(8,128)S(1)}, f32[2,8,128,128]{3,2,1,0:T(8,128)S(1)}) conditional(s32[]{:T(128)} %convert_element_type.167, (s32[]{:T(128)}, s32[]{:T(128)}, bf16[8192,256]{0,1:T(8,128)(2,1)}, bf16[128,2,8,128]{3,0,2,1:T(8,128)(2,1)S(1)}, f32[2,8,128]{2,1,0:T(8,128)S(1)}, ...), branch_computations={%region_5.7_spmd, %region_8.8_spmd} | conditional | flops 551096960 | bytes 17159750 | solution.py:144
  291.5 4.8 %conditional.3 = (f32[2,8,128]{2,1,0:T(8,128)S(1)}, f32[2,8,128]{2,1,0:T(8,128)S(1)}, f32[2,8,128,128]{3,2,1,0:T(8,128)S(1)}) conditional(s32[]{:T(128)} %convert_element_type.167, (s32[]{:T(128)}, s32[]{:T(128)}, bf16[8192,256]{0,1:T(8,128)(2,1)}, bf16[128,2,8,128]{3,0,2,1:T(8,128)(2,1)S(1)}, f32[2,8,128]{2,1,0:T(8,128)S(1)}, ...), branch_computations={%region_5.7_spmd, %region_8.8_spmd} | conditional | flops 551096960 | bytes 17159750 | solution.py:144
  296.4 4.8 %conditional.3 = (f32[2,8,128]{2,1,0:T(8,128)S(1)}, f32[2,8,128]{2,1,0:T(8,128)S(1)}, f32[2,8,128,128]{3,2,1,0:T(8,128)S(1)}) conditional(s32[]{:T(128)} %convert_element_type.167, (s32[]{:T(128)}, s32[]{:T(128)}, bf16[8192,256]{0,1:T(8,128)(2,1)}, bf16[128,2,8,128]{3,0,2,1:T(8,128)(2,1)S(1)}, f32[2,8,128]{2,1,0:T(8,128)S(1)}, ...), branch_computations={%region_5.7_spmd, %region_8.8_spmd} | conditional | flops 551096960 | bytes 17159750 | solution.py:144
  301.3 8.8 %multiply_reduce_fusion = (f32[128]{0:T(128)S(1)}, f32[16,128,128]{2,1,0:T(8,128)}) fusion(f32[16,128,128]{2,1,0:T(8,128)} %convolution_add_fusion.2, f32[128,16]{0,1:T(8,128)S(1)} %get-tuple-element.395, f32[4,16,128,128]{3,2,1,0:T(8,128)} %all-gather.11.cloned.1.call-done, f32[8,16,128,128]{3,2,1,0:T(8,128)} %all-gather.9.cloned.1.call-done, ...), kind=kOutput, calls=%fused_computation.72 | convolution fusion | flops 81264512 | bytes 17311246 | tf_op jit(solution)/shard_map/thd,hde->the/dot_general | solution.py:105
  (249 shorter events, 115.0 us)
Async XLA Ops:
  7.2 24.4 %all-gather.15.cloned.1.call-start = ((), (), s32[]{:S(2)}) async-start(), calls=%async_computation.4 | async-start | bytes 3145728 | tf_op jit(solution)/shard_map/all_gather | solution.py:29
  9.8 3.2 copy-start.5
  9.8 3.3 %copy-start.9 = (u32[256]{0:T(256)S(1)}, u32[256]{0:T(256)}, u32[]{:S(2)}) copy-start(u32[256]{0:T(256)} %constant.137) | copy-start | bytes 3076
  9.8 3.9 %copy-start.8 = (u32[256]{0:T(256)S(1)}, u32[256]{0:T(256)}, u32[]{:S(2)}) copy-start(u32[256]{0:T(256)} %constant.142) | copy-start | bytes 3076
  10.1 24.2 %copy-start.2 = (bf16[128,2048]{0,1:T(8,128)(2,1)}, bf16[128,2048]{0,1:T(8,128)(2,1)S(1)}, u32[]{:S(2)}) copy-start(bf16[128,2048]{0,1:T(8,128)(2,1)S(1)} %copy.102) | copy-start | bytes 1572868
  10.1 24.3 %copy-start.3 = (bf16[128,256]{1,0:T(8,128)(2,1)S(1)}, bf16[128,256]{1,0:T(8,128)(2,1)}, u32[]{:S(2)}) copy-start(bf16[128,256]{1,0:T(8,128)(2,1)} %param.21) | copy-start | bytes 196612
  12.9 21.7 %copy-start.4 = (bf16[128,256]{1,0:T(8,128)(2,1)S(1)}, bf16[128,256]{1,0:T(8,128)(2,1)}, u32[]{:S(2)}) copy-start(bf16[128,256]{1,0:T(8,128)(2,1)} %param.22) | copy-start | bytes 196612
  12.9 115.2 %all-gather.9.cloned.1.call-start = ((), (), s32[]{:S(2)}) async-start(), calls=%async_computation.1 | async-start | bytes 9437184 | tf_op jit(solution)/shard_map/all_gather | solution.py:29
  34.4 182.4 %all-gather.13.cloned.1.call-start = ((), (), s32[]{:S(2)}) async-start(), calls=%async_computation.3 | async-start | bytes 8519680 | tf_op jit(solution)/shard_map/all_gather | solution.py:53
  35.4 265.9 %all-gather.11.cloned.1.call-start = ((), (), s32[]{:S(2)}) async-start(), calls=%async_computation.2 | async-start | bytes 5242880 | tf_op jit(solution)/shard_map/all_gather | solution.py:29
  128.1 5.2 %copy-start = (bf16[128,2048]{1,0:T(8,128)(2,1)S(1)}, bf16[128,2048]{1,0:T(8,128)(2,1)}, u32[]{:S(2)}) copy-start(bf16[128,2048]{1,0:T(8,128)(2,1)} %param.18) | copy-start | bytes 1572868
  133.2 1.3 copy-start.1
  145.2 3.4 %copy-start.7 = (bf16[128,2048]{1,0:T(8,128)(2,1)S(1)}, bf16[128,2048]{1,0:T(8,128)(2,1)}, u32[]{:S(2)}) copy-start(bf16[128,2048]{1,0:T(8,128)(2,1)} %param.14) | copy-start | bytes 1572868
  301.3 18.9 %copy-start.6 = (f32[2048]{0:T(1024)S(1)}, f32[2048]{0:T(1024)}, u32[]{:S(2)}) copy-start(f32[2048]{0:T(1024)} %param.19) | copy-start | bytes 24580
  310.7 9.5 %all-to-all-start = ((f32[4,1,128]{2,1,0:T(1,128)}), f32[4,1,128]{2,1,0:T(1,128)S(1)}, u32[]{:S(2)}, u32[]{:S(2)}) async-start(f32[4,1,128]{2,1,0:T(1,128)} %broadcast_in_dim.97), calls=%async_computation | async-start | bytes 4096 | tf_op jit(solution)/shard_map/all_to_all | solution.py:41
Sparse Core Ops, SparseCore 0:
  13.0 18.5 all-gather.14
  34.5 93.5 all-gather.8
  131.2 85.4 all-gather.12
  218.4 51.0 all-gather.10
where the time goes:
time: 330 us; the launch traced here: 329 us
  waiting for transfers between devices  159 us (48%)
  matrix products  58.2 us (18%)
  other arithmetic  32.3 us (10%)
  local copies, waits for them, and re-layouts  29.1 us (9%)
  blocking collectives  28.6 us (9%)
  between operations  15.9 us (5%)
  starting transfers between devices  4.41 us (1%)
    all_gather x3, waiting for transfers between devices, carried_in(): pieces = jax.tree.map(lambda part: lax.all_gather(part, axis), subtotal)  89.7 us
    all_gather x1, waiting for transfers between devices, in_one_piece(): whole = lax.all_gather(both, axis, axis=dim, tiled=True)  65.3 us
    dot_general x16, matrix products, update(): jnp.einsum('kgts,skd->kgtd', probs.astype(jnp.bfloat16), vparts, preferre...  27 us
    unnamed x2, blocking collectives  18.7 us
    dynamic_slice x16, local copies, waits for them, and re-layouts, loop_body(): vslice = lax.dynamic_slice_in_dim(vpiece, offset, stride, 0)  17.2 us
    reduce_sum x16, other arithmetic, update(): den_new = den * alpha + jnp.sum(probs, axis=-1)  16 us
    dot_general x16, matrix products, update(): jnp.einsum('tkgd,skd->kgts', qgroup, kparts, preferred_element_type=jnp.f...  13.4 us
    all_gather x1, blocking collectives, carried_in(): pieces = jax.tree.map(lambda part: lax.all_gather(part, axis), subtotal)  9.88 us
  transfers between devices with their start and end apart: 5, of which 4 were waited for; matrix products, arithmetic and copies ran while one was open for 30% of the time, Pallas kernels for 0%

commit v1 on v0

v1 whole, which is shorter than its diff:
```python
import functools
import math

import jax
import jax.numpy as jnp
from jax import lax
from jax.experimental import pallas as pl
from jax.experimental.pallas import tpu as pltpu
from jax.sharding import Mesh
from jax.sharding import PartitionSpec as P

HD = 128
TOK = 128
HEADS = 16
HALF = 8
WIDTH = HEADS * HD
GROUP = 8
EPS = 1e-06
SCALE2 = math.log2(math.e) / math.sqrt(HD)
NEG = -1e30
MESH = pl.DeviceIdType.MESH
BF = jnp.bfloat16
F32 = jnp.float32
NY, NZ = 4, 8
UNITS = NY * NZ
STEP_UNITS = 4
SHARDS = 2 * STEP_UNITS
KEYS = SHARDS * TOK
STEPS = UNITS // STEP_UNITS
CHUNKS = 2 * STEPS


def ring_next(r, size, tie_up):
    r = r % size
    half = size // 2

    def wanted(distance, up):
        return distance < half or (distance == half and up == tie_up)

    if r == 0:
        return [s for s, up in ((-1, True), (1, False)) if wanted(1, up)]
    if r < half or (r == half and tie_up):
        return [-1] if wanted(r + 1, True) else []
    return [1] if wanted(size - r + 1, False) else []


def sends_of(block):
    dy, dz = block
    out = []
    if dy == 0:
        out += [("z", s) for s in ring_next(dz, NZ, True)]
    out += [("y", s) for s in ring_next(dy, NY, dz % 2 == 0)]
    return out


def plan():
    wire, hop, tick, first = 2.8, 1.8, 2.3, 0.0
    arrival = {(0, 0): 0.0}
    free = {("z", -1): 0.0, ("z", 1): 0.0, ("y", -1): 0.0, ("y", 1): 0.0}
    waiting = {key: [] for key in free}
    held, order, chunks = set(), [], []
    k = 0
    while len(held) < UNITS or any(waiting.values()):
        now = first + k * tick
        waits, starts = [], []
        ready = sorted((b for b in arrival if b not in held and arrival[b] <= now), key=lambda b: arrival[b])
        for b in ready:
            held.add(b)
            order.append(b)
            waits.append(b)
            for way in sends_of(b):
                waiting[way].append(b)
        for way, queue in waiting.items():
            while queue and free[way] < now + tick:
                b = queue.pop(0)
                axis, s = way
                dy, dz = b
                target = ((dy - s) % NY, dz) if axis == "y" else (dy, (dz - s) % NZ)
                free[way] = max(free[way], now) + wire
                arrival[target] = free[way] + hop
                starts.append((b, way, target))
        chunks.append((waits, starts))
        k += 1
    return order, chunks


ORDER, PLAN = plan()
UNIT_AT = {block: place for place, block in enumerate(ORDER)}


def schedule():
    held_at = {b: k for k, (waits, _) in enumerate(PLAN) for b in waits}
    ahead = [([], []) for _ in range(CHUNKS + 1)]
    k = 0
    for c in range(CHUNKS):
        step = c // 2
        need = max(held_at[b] for b in ORDER[step * STEP_UNITS : (step + 1) * STEP_UNITS])
        last = max(need, c)
        while k <= last and k < len(PLAN):
            ahead[c][0].append(k)
            k += 1
    while k < len(PLAN):
        ahead[CHUNKS][0].append(k)
        k += 1
    return [a[0] for a in ahead]


AHEAD = schedule()


def kernel(
    q_hbm, k_hbm, v_hbm, gate_hbm, queries_hbm, keys_hbm, values_hbm, decay_ref, gain_ref, order_ref,
    mixed_ref, attended_ref,
    qx, kx, vx, gx, qs, buf, qaug, kaug, vaug, top, acc, cum, state, dec, lin,
    s_out, s_in, z_out, z_in, edge, y_out, y_in, p_out, p_in, c_out, carr_a, carr_b, x_out, x_in,
    shard_of, load_sem, kv_load_sem, recv_sem, send_sem, part_sem, small_send, small_recv,
):
    me_y, me_z, me_c, me_x = (lax.axis_index(n) for n in ("y", "z", "c", "x"))
    other = 1 - me_c
    first = me_c == 0

    def at(y=None, z=None, c=None, x=None):
        return (
            me_y if y is None else lax.rem(me_y + y + NY, NY),
            me_z if z is None else lax.rem(me_z + z + NZ, NZ),
            me_c if c is None else other,
            me_x if x is None else lax.rem(me_x + x + 4, 4),
        )

    peers = [at(z=d) for d in range(1, NZ)] + [at(y=d) for d in range(1, NY)]
    peers += [at(x=d) for d in range(1, 4)] + [at(c=1)]

    loads = [
        pltpu.make_async_copy(src, dst, load_sem.at[n])
        for n, (src, dst) in enumerate(
            ((k_hbm, kx), (v_hbm, vx), (q_hbm, qx), (queries_hbm, qs), (gate_hbm, gx))
        )
    ]
    kv_loads = []
    for n, src in enumerate((keys_hbm, values_hbm)):
        for g in range(2):
            kv_loads.append(
                pltpu.make_async_copy(
                    src.at[:, g * HD : (g + 1) * HD], buf.at[0, 2 * n + g], kv_load_sem.at[2 * n + g]
                )
            )
    barrier = pltpu.get_barrier_semaphore()
    for peer in peers:
        pl.semaphore_signal(barrier, inc=1, device_id=peer, device_id_type=MESH)
    for load in kv_loads + loads:
        load.start()

    def remote(src, dst, send, recv, device):
        return pltpu.make_async_remote_copy(
            src_ref=src, dst_ref=dst, send_sem=send, recv_sem=recv, device_id=device, device_id_type=MESH
        )

    send_place = {}
    for _, starts in PLAN:
        for b, way, target in starts:
            send_place[(b, way)] = len(send_place)

    def block_copy(b, way, target):
        axis, s = way
        device = at(y=s) if axis == "y" else at(z=s)
        return remote(
            buf.at[2 * UNIT_AT[b]], buf.at[2 * UNIT_AT[target]],
            send_sem.at[send_place[(b, way)]], recv_sem.at[2 * UNIT_AT[target]], device,
        )

    def partner_copy(b):
        u = UNIT_AT[b]
        return remote(buf.at[2 * u], buf.at[2 * u + 1], part_sem.at[u], recv_sem.at[2 * u + 1], at(c=1))

    def arrived(place):
        return remote(buf.at[place], buf.at[place], part_sem.at[0], recv_sem.at[place], at(c=1))

    def communicate(k):
        waits, starts = PLAN[k]
        for b in waits:
            if b != (0, 0):
                arrived(2 * UNIT_AT[b]).wait_recv()
            partner_copy(b).start()
        for b, way, target in starts:
            block_copy(b, way, target).start()

    x = decay_ref[...]
    lane = lax.broadcasted_iota(jnp.int32, (HEADS, TOK), 1)
    for s in (1, 2, 4, 8, 16, 32, 64):
        x = x + jnp.where(lane >= s, pltpu.roll(x, s, axis=1), 0.0)
    cum[...] = x

    row_i = lax.broadcasted_iota(jnp.int32, (TOK, TOK), 0)
    col_i = lax.broadcasted_iota(jnp.int32, (TOK, TOK), 1)
    lower = row_i >= col_i
    head_rows = lax.broadcasted_iota(jnp.int32, (16, HD), 0)

    def columns(h):
        return pl.ds(pl.multiple_of(h * HD, HD), HD)

    def cum_of(h):
        rows = jnp.broadcast_to(cum[pl.ds(h, 1), :], (TOK, TOK))
        return rows, jnp.transpose(rows)

    def silu(v):
        v = v.astype(F32)
        return (v / (1.0 + jnp.exp(-v))).astype(BF)

    def pack_decay(d):
        hi = d.astype(BF)
        rest = d - hi.astype(F32)
        mid = rest.astype(BF)
        low = (rest - mid.astype(F32)).astype(BF)
        return jnp.where(
            head_rows == 0, hi.astype(F32), jnp.where(head_rows == 1, mid.astype(F32), low.astype(F32))
        ).astype(BF)

    def unpack_decay(rows):
        r = rows.astype(F32)
        return r[0:1] + r[1:2] + r[2:3]

    loads[0].wait()
    loads[1].wait()

    def local_state(h, carry):
        cols = columns(h)
        _, cb = cum_of(h)
        kb = silu(kx[:, cols])
        vb = silu(vx[:, cols])
        kx[:, cols] = kb
        vx[:, cols] = vb
        last = cb[TOK - 1 : TOK, :]
        kdec = (kb.astype(F32) * jnp.exp(last - cb)).astype(BF)
        s = lax.dot_general(kdec, vb, (((0,), (0,)), ((), ())), preferred_element_type=F32)
        state[h] = s
        d = jnp.exp(last)
        dec[h] = jnp.broadcast_to(d, (8, HD))
        return carry

    lax.fori_loop(0, HEADS, local_state, 0)

    def to_partner(r, carry):
        h = other * HALF + r
        s_out[r, 0:HD] = state[h].astype(BF)
        s_out[r, HD : HD + 16] = pack_decay(dec[h][0:1])
        return carry

    lax.fori_loop(0, HALF, to_partner, 0)
    pl.semaphore_wait(barrier, len(peers))
    state_copy = remote(s_out, s_in, small_send.at[0], small_recv.at[0], at(c=1))
    state_copy.start()
    for load in kv_loads:
        load.wait()
    communicate(0)

    loads[3].wait()
    unit = jnp.where(row_i == col_i, 1.0, 0.0).astype(BF)

    def spread(h, carry):
        rows = pl.ds(pl.multiple_of(h * TOK, TOK), TOK)
        qaug[rows, 0:HD] = qs[:, columns(h)]
        qaug[rows, HD : 2 * HD] = unit
        top[rows, :] = jnp.full((TOK, HD), NEG, F32)
        acc[rows, :] = jnp.zeros((TOK, 2 * HD), F32)
        return carry

    lax.fori_loop(0, HEADS, spread, 0)
    for u, (dy, dz) in enumerate(ORDER):
        chip = lax.rem(me_y + dy, NY) * NZ + lax.rem(me_z + dz, NZ)
        shard_of[2 * u] = 2 * chip + me_c
        shard_of[2 * u + 1] = 2 * chip + other
    my_shard = order_ref[0]
    above = jnp.where(row_i > col_i, NEG, 0.0)

    def softmax(i):
        g = lax.rem(i, 2)
        base = lax.div(i, 2) * SHARDS
        for s in range(SHARDS):
            rows = slice(s * TOK, (s + 1) * TOK)
            shard = shard_of[base + s]
            kaug[rows, 0:HD] = buf[base + s, g]
            vaug[rows, :] = buf[base + s, 2 + g]
            whole = jnp.where(shard > my_shard, NEG, 0.0)
            part = jnp.where(shard == my_shard, 1.0, 0.0)
            kaug[rows, HD : 2 * HD] = (above * part + whole).astype(BF)
        rows = pl.ds(pl.multiple_of(g * GROUP * TOK, GROUP * TOK), GROUP * TOK)
        sc = lax.dot_general(
            qaug[rows, :], kaug[...], (((1,), (1,)), ((), ())), preferred_element_type=F32
        )
        old = top[rows, :]
        new = jnp.maximum(old, jnp.max(sc, axis=1, keepdims=True))
        w = jnp.exp2(sc * SCALE2 - jnp.tile(new * SCALE2, (1, SHARDS)))
        alpha = jnp.exp2((old - new) * SCALE2)
        pv = jnp.dot(w.astype(BF), vaug[...], preferred_element_type=F32)
        acc[rows, 0:HD] = acc[rows, 0:HD] * alpha + pv
        den = w[:, 0:HD]
        for s in range(1, SHARDS):
            den = den + w[:, s * HD : (s + 1) * HD]
        acc[rows, HD : 2 * HD] = acc[rows, HD : 2 * HD] * alpha + den
        top[rows, :] = new

    def intra():
        loads[2].wait()

        def one(h, carry):
            cols = columns(h)
            rb, cb = cum_of(h)
            qb = silu(qx[:, cols])
            sc = lax.dot_general(qb, kx[:, cols], (((1,), (1,)), ((), ())), preferred_element_type=F32)
            decay = jnp.where(lower, jnp.exp(jnp.where(lower, cb - rb, 0.0)), 0.0)
            w = (sc * decay).astype(BF)
            lin[:, cols] = jnp.dot(w, vx[:, cols], preferred_element_type=F32)
            qx[:, cols] = (qb.astype(F32) * jnp.exp(cb)).astype(BF)
            return carry

        lax.fori_loop(0, HEADS, one, 0)

    def z_copy(d):
        head = lax.rem(me_z + d, NZ)
        return remote(z_out.at[head], z_in.at[NZ - d], small_send.at[d], small_recv.at[NZ - d], at(z=d))

    def z_arrival(d):
        return remote(z_out.at[0], z_in.at[d], small_send.at[0], small_recv.at[d], at(z=d))

    def chip_totals():
        remote(s_out, s_in, small_send.at[0], small_recv.at[0], at(c=1)).wait_recv()

        def one(r, carry):
            h = me_c * HALF + r
            mine, d_mine = state[h], dec[h][0:1]
            theirs = s_in[r, 0:HD].astype(F32)
            d_theirs = unpack_decay(s_in[r, HD : HD + 16])
            total = jnp.where(first, d_theirs, 1.0) * mine + jnp.where(first, 1.0, d_mine) * theirs
            z_out[r, 0:HD] = total.astype(BF)
            z_out[r, HD : HD + 16] = pack_decay(d_mine * d_theirs)
            return carry

        lax.fori_loop(0, HALF, one, 0)
        for d in range(1, NZ):
            z_copy(d).start()

    def y_copy(d):
        return remote(y_out, y_in.at[NY - d], small_send.at[8 + d], small_recv.at[8 + NY - d], at(y=d))

    def y_arrival(d):
        return remote(y_out, y_in.at[d], small_send.at[0], small_recv.at[8 + d], at(y=d))

    def row_scan():
        for d in range(1, NZ):
            z_arrival(d).wait_recv()
        z_in[0] = z_out[me_z]

        def one(k, carry):
            e, a = carry
            rel = lax.rem(k - me_z + NZ, NZ)
            edge[k, 0:HD] = e
            edge[k, HD : HD + 8] = jnp.broadcast_to(a, (8, HD))
            d = unpack_decay(z_in[rel, HD : HD + 16])
            return d * e + z_in[rel, 0:HD].astype(F32), a * d

        e, a = lax.fori_loop(0, NZ, one, (jnp.zeros((HD, HD), F32), jnp.ones((1, HD), F32)))
        y_out[0:HD] = e
        y_out[HD : HD + 8] = jnp.broadcast_to(a, (8, HD))
        y_in[0] = jnp.zeros((HD + 8, HD), F32)
        for d in range(1, NY):
            y_copy(d).start()

    def p_copy(d):
        chip = lax.rem(me_z + d, NZ)
        return remote(p_out.at[chip], p_in.at[NZ - d], small_send.at[16 + d], small_recv.at[16 + NZ - d], at(z=d))

    def p_arrival(d):
        return remote(p_out.at[0], p_in.at[d], small_send.at[0], small_recv.at[16 + d], at(z=d))

    def prefixes():
        for d in range(1, NY):
            y_arrival(d).wait_recv()
        carry = jnp.zeros((HD, HD), F32)
        for k in range(NY - 1):
            rel = lax.rem(k - me_y + NY, NY)
            grown = y_in[rel, HD : HD + 1] * carry + y_in[rel, 0:HD]
            carry = jnp.where(k < me_y, grown, carry)

        for k in range(NZ):
            p_out[k] = (edge[k, 0:HD] + edge[k, HD : HD + 1] * carry).astype(BF)
        for d in range(1, NZ):
            p_copy(d).start()

    def carries():
        for d in range(1, NZ):
            p_arrival(d).wait_recv()
        p_in[0] = p_out[me_z]

        def one(r, carry):
            h = me_c * HALF + r
            before = p_in[lax.rem(r - me_z + NZ, NZ)].astype(F32)
            d_theirs = unpack_decay(s_in[r, HD : HD + 16])
            d = jnp.where(first, dec[h][0:1], d_theirs)
            s = jnp.where(first, state[h], s_in[r, 0:HD].astype(F32))
            after = d * before + s
            carr_a[r] = jnp.where(first, before, after).astype(BF)
            c_out[r] = jnp.where(first, after, before).astype(BF)
            return carry

        lax.fori_loop(0, HALF, one, 0)
        remote(c_out, carr_b, small_send.at[24], small_recv.at[24], at(c=1)).start()

    def x_copy(d):
        return remote(x_out, x_in.at[4 - d], small_send.at[24 + d], small_recv.at[24 + 4 - d], at(x=d))

    def x_arrival(d):
        return remote(x_out, x_in.at[d], small_send.at[0], small_recv.at[24 + d], at(x=d))

    def inter():
        def half(source, start):
            def one(r, total):
                cols = columns(start + r)
                value = lin[:, cols] + jnp.dot(qx[:, cols], source[r], preferred_element_type=F32)
                lin[:, cols] = value
                return total + value * value

            return one

        total = lax.fori_loop(0, HALF, half(carr_a, me_c * HALF), jnp.zeros((TOK, HD), F32))
        remote(c_out, carr_b, small_send.at[24], small_recv.at[24], at(c=1)).wait_recv()
        total = lax.fori_loop(0, HALF, half(carr_b, other * HALF), total)
        x_out[...] = total
        for d in range(1, 4):
            x_copy(d).start()

    def finish():
        loads[4].wait()
        total = x_out[...]
        for d in range(1, 4):
            x_arrival(d).wait_recv()
            total = total + x_in[d]
        inv = lax.rsqrt(jnp.sum(total, axis=1, keepdims=True) / (4 * WIDTH) + EPS)
        inv = jnp.broadcast_to(inv, (TOK, HD))

        def one(h, carry):
            cols = columns(h)
            g = gx[:, cols].astype(F32)
            gated = 1.0 / (1.0 + jnp.exp(-g))
            mixed_ref[:, cols] = (lin[:, cols] * inv * gain_ref[:, cols] * gated).astype(BF)
            return carry

        lax.fori_loop(0, HEADS, one, 0)

    TASKS = {0: intra, 1: chip_totals, 4: row_scan, 7: prefixes, 10: carries, 12: inter, 14: finish}

    def chunk(i, carry):
        for c in range(CHUNKS):

            @pl.when(i == c)
            def _(c=c):
                for k in AHEAD[c]:
                    if k > 0:
                        communicate(k)
                if c % 2 == 0:
                    for u in range(c // 2 * STEP_UNITS, (c // 2 + 1) * STEP_UNITS):
                        arrived(2 * u + 1).wait_recv()
                if c in TASKS:
                    TASKS[c]()

        softmax(i)
        return carry

    lax.fori_loop(0, CHUNKS, chunk, 0)
    for k in AHEAD[CHUNKS]:
        communicate(k)

    def result(h, carry):
        rows = pl.ds(pl.multiple_of(h * TOK, TOK), TOK)
        den = jnp.sum(acc[rows, HD : 2 * HD], axis=1, keepdims=True)
        attended_ref[:, columns(h)] = (acc[rows, 0:HD] / den).astype(BF)
        return carry

    lax.fori_loop(0, HEADS, result, 0)

    state_copy.wait_send()
    for d in range(1, NZ):
        z_copy(d).wait_send()
        p_copy(d).wait_send()
    for d in range(1, NY):
        y_copy(d).wait_send()
    remote(c_out, carr_b, small_send.at[24], small_recv.at[24], at(c=1)).wait_send()
    for d in range(1, 4):
        x_copy(d).wait_send()
    for waits, starts in PLAN:
        for b in waits:
            partner_copy(b).wait_send()
        for b, way, target in starts:
            block_copy(b, way, target).wait_send()


def body(q_lin, k_lin, v_lin, log_decay, gate, norm_gain, queries, keys, values, order):
    vmem = pl.BlockSpec(memory_space=pltpu.VMEM)
    hbm = pl.BlockSpec(memory_space=pl.ANY)
    out = jax.ShapeDtypeStruct((TOK, WIDTH), BF)
    n_sends = sum(len(starts) for _, starts in PLAN)
    wide = pltpu.VMEM((TOK, WIDTH), BF)
    return pl.pallas_call(
        kernel,
        out_shape=(out, out),
        in_specs=[hbm] * 7 + [vmem, vmem, pl.BlockSpec(memory_space=pltpu.SMEM)],
        out_specs=(vmem, vmem),
        scratch_shapes=[
            wide, wide, wide, wide, wide,
            pltpu.VMEM((2 * UNITS, 4, TOK, HD), BF),
            pltpu.VMEM((HEADS * TOK, 2 * HD), BF),
            pltpu.VMEM((KEYS, 2 * HD), BF),
            pltpu.VMEM((KEYS, HD), BF),
            pltpu.VMEM((HEADS * TOK, HD), F32),
            pltpu.VMEM((HEADS * TOK, 2 * HD), F32),
            pltpu.VMEM((HEADS, TOK), F32),
            pltpu.VMEM((HEADS, HD, HD), F32),
            pltpu.VMEM((HEADS, 8, HD), F32),
            pltpu.VMEM((TOK, WIDTH), F32),
            pltpu.VMEM((HALF, HD + 16, HD), BF),
            pltpu.VMEM((HALF, HD + 16, HD), BF),
            pltpu.VMEM((NZ, HD + 16, HD), BF),
            pltpu.VMEM((NZ, HD + 16, HD), BF),
            pltpu.VMEM((NZ, HD + 8, HD), F32),
            pltpu.VMEM((HD + 8, HD), F32),
            pltpu.VMEM((NY, HD + 8, HD), F32),
            pltpu.VMEM((NZ, HD, HD), BF),
            pltpu.VMEM((NZ, HD, HD), BF),
            pltpu.VMEM((HALF, HD, HD), BF),
            pltpu.VMEM((HALF, HD, HD), BF),
            pltpu.VMEM((HALF, HD, HD), BF),
            pltpu.VMEM((TOK, HD), F32),
            pltpu.VMEM((4, TOK, HD), F32),
            pltpu.SMEM((2 * UNITS,), jnp.int32),
            pltpu.SemaphoreType.DMA((5,)),
            pltpu.SemaphoreType.DMA((4,)),
            pltpu.SemaphoreType.DMA((2 * UNITS,)),
            pltpu.SemaphoreType.DMA((n_sends,)),
            pltpu.SemaphoreType.DMA((UNITS,)),
            pltpu.SemaphoreType.DMA((28,)),
            pltpu.SemaphoreType.DMA((28,)),
        ],
        compiler_params=pltpu.CompilerParams(
            collective_id=0, has_side_effects=True, vmem_limit_bytes=62 * 2**20
        ),
    )(
        q_lin, k_lin, v_lin, gate, queries, keys, values, log_decay, norm_gain.reshape(1, WIDTH), order
    )


def solution(mesh):
    finer = Mesh(
        mesh.devices.reshape(NY, NZ, 2, mesh.shape["head"]), ("y", "z", "c", "x")
    )
    rows = ("y", "z", "c")
    tile = P(rows, "x")
    return jax.shard_map(
        body,
        mesh=finer,
        in_specs=(tile, tile, tile, P("x", rows), tile, P("x"), tile, tile, tile, P(rows)),
        out_specs=(tile, tile),
        check_vma=False,
    )
```

time: 330 us -> 87.3 us (0.26)
  the two profiles are of different devices: /device:TPU:32 before, /device:TPU:1 now
where the time goes in v1:
time: 87.3 us; the launch traced here: 87.1 us
  Pallas kernels  83.1 us (95%)
  local copies, waits for them, and re-layouts  2.74 us (3%)
  between operations  1.3 us (1%)
    pallas_call x1, Pallas kernels, body(): pl.pallas_call(kernel, out_shape=(out, out), in_specs=[hbm] * 7 + [vmem,...  83.1 us
    unnamed x4, local copies, waits for them, and re-layouts  2.74 us

profile of v1, /device:TPU:1, one launch (start us, length us, event | category | flops | bytes accessed | tf_op | source)
XLA Modules:
  0.0 87.1 jit_solution(8870504624182039056)
XLA Ops:
  1.3 83.1 %shard_map.113 = (bf16[128,2048]{1,0:T(8,128)(2,1)}, bf16[128,2048]{1,0:T(8,128)(2,1)}) custom-call(bf16[128,2048]{1,0:T(8,128)(2,1)} %q_hbm.1, bf16[128,2048]{1,0:T(8,128)(2,1)} %k_hbm.1, bf16[128,2048]{1,0:T(8,128)(2,1)} %v_hbm.1, bf16[128,2048]{1,0:T(8,128)(2,1)} %gate_hbm.1, bf16[128,2048]{1,0:T(8,128)(2,1)} %queries_hbm.1, bf16[128,256]{1,0:T(8,128)(2,1)} %keys_hbm.1, ...), custom_call_target="tpu_custom_call" | custom-call | tf_op jit(solution)/shard_map/pallas_call | solution.py:502
  84.4 0.0 copy-start
  84.4 1.9 %copy.15 = bf16[128,2048]{1,0:T(8,128)(2,1)} copy(bf16[128,2048]{1,0:T(8,128)(2,1)} %get-tuple-element.4) | data formatting | bytes 1048576
  86.3 0.0 copy-done
  86.3 0.8 copy.16
Async XLA Ops:
  84.4 2.0 %copy-start = (bf16[128,2048]{1,0:T(8,128)(2,1)S(1)}, bf16[128,2048]{1,0:T(8,128)(2,1)}, u32[]{:S(2)}) copy-start(bf16[128,2048]{1,0:T(8,128)(2,1)} %get-tuple-element.5) | copy-start | bytes 1572868

commit v2 on v1

--- a/solution.py
+++ b/solution.py
@@ -44,68 +44,118 @@
     return [1] if wanted(size - r + 1, False) else []
 
 
-def sends_of(block):
-    dy, dz = block
+PART_SIZES = (4,)
+RATE, LATENCY = 104.0, 1.8
+CORE_RATE, CORE_LATENCY = 400.0, 1.1
+SOFTMAX, ISSUE, AHEAD_TIME = 1.9, 0.04, 2.0
+COST = {"intra": 2.0, "chip_totals": 0.7, "row_scan": 0.7, "prefixes": 0.4, "carries": 0.7, "inter": 1.2, "finish": 0.6}
+MESSAGES = {
+    "chip_totals": [(("z", 1), 36 * 8), (("z", -1), 36 * 8)],
+    "row_scan": [(("y", 1), 70 * 2), (("y", -1), 70 * 2)],
+    "prefixes": [(("z", 1), 32 * 8), (("z", -1), 32 * 8)],
+    "carries": [(("c", 0), 256)],
+    "inter": [(("x", 1), 64 * 2)],
+    "finish": [],
+}
+
+
+def sends_of(item):
+    part, dy, dz = item
     out = []
-    if dy == 0:
-        out += [("z", s) for s in ring_next(dz, NZ, True)]
-    out += [("y", s) for s in ring_next(dy, NY, dz % 2 == 0)]
+    if part == 0:
+        if dy == 0:
+            out += [("z", s) for s in ring_next(dz, NZ, True)]
+        out += [("y", s) for s in ring_next(dy, NY, dz % 2 == 0)]
+    else:
+        if dz == 0:
+            out += [("y", s) for s in ring_next(dy, NY, True)]
+        out += [("z", s) for s in ring_next(dz, NZ, dy % 2 == 0)]
     return out
 
 
 def plan():
-    wire, hop, tick, first = 2.8, 1.8, 2.3, 0.0
-    arrival = {(0, 0): 0.0}
-    free = {("z", -1): 0.0, ("z", 1): 0.0, ("y", -1): 0.0, ("y", 1): 0.0}
-    waiting = {key: [] for key in free}
-    held, order, chunks = set(), [], []
-    k = 0
-    while len(held) < UNITS or any(waiting.values()):
-        now = first + k * tick
-        waits, starts = [], []
-        ready = sorted((b for b in arrival if b not in held and arrival[b] <= now), key=lambda b: arrival[b])
-        for b in ready:
-            held.add(b)
-            order.append(b)
-            waits.append(b)
-            for way in sends_of(b):
-                waiting[way].append(b)
-        for way, queue in waiting.items():
-            while queue and free[way] < now + tick:
-                b = queue.pop(0)
+    parts = range(len(PART_SIZES))
+    free = {}
+    arrival = {}
+    queues = {(axis, s): [] for axis in "zy" for s in (-1, 1)}
+    held, order, chunks, ops = set(), [], [], []
+    pending = ["intra"] + list(MESSAGES)
+    due = {"intra": 0.0}
+    now = 0.0
+
+    def use(way, size):
+        rate, latency = (CORE_RATE, CORE_LATENCY) if way[0] == "c" else (RATE / 2, LATENCY)
+        free[way] = max(free.get(way, 0.0), now) + size * 1.024 / rate
+        return free[way] + latency
+
+    def issue():
+        for way, queue in queues.items():
+            while queue and free.get(way, 0.0) < now + AHEAD_TIME:
+                item = queue.pop(0)
                 axis, s = way
-                dy, dz = b
-                target = ((dy - s) % NY, dz) if axis == "y" else (dy, (dz - s) % NZ)
-                free[way] = max(free[way], now) + wire
-                arrival[target] = free[way] + hop
-                starts.append((b, way, target))
-        chunks.append((waits, starts))
-        k += 1
+                part, dy, dz = item
+                target = (part, (dy - s) % NY, dz) if axis == "y" else (part, dy, (dz - s) % NZ)
+                arrival[target] = use(way, 32 * PART_SIZES[part])
+                ops.append(("start", item, way, target))
+
+    def take(item):
+        held.add(item)
+        for way in sends_of(item):
+            queues[way].append(item)
+        issue()
+        arrival[item + (1,)] = use(("c", 0), 32 * PART_SIZES[item[0]])
+        ops.append(("partner", item))
+        if all((p,) + item[1:] in held for p in parts):
+            order.append(item[1:])
+
+    due["chip_totals"] = use(("c", 0), 288)
+    for p in parts:
+        ops.append(("take", (p, 0, 0)))
+        take((p, 0, 0))
+    done = 0
+    while done < CHUNKS or pending:
+        while True:
+            if pending and due.get(pending[0], 1e9) <= now:
+                name = pending.pop(0)
+                ops.append(("task", name))
+                now += COST[name]
+                if pending:
+                    sent = [use(way, size) for way, size in MESSAGES.get(name, [])]
+                    if sent:
+                        due[pending[0]] = max(sent)
+                continue
+            came = sorted((i for i in arrival if len(i) == 3 and i not in held and arrival[i] <= now), key=lambda i: arrival[i])
+            if came:
+                now += ISSUE
+                ops.append(("take", came[0]))
+                take(came[0])
+                continue
+            break
+        issue()
+        group = order[done // 2 * STEP_UNITS : (done // 2 + 1) * STEP_UNITS]
+        needs = [(p,) + b + (1,) for b in group for p in parts]
+        if done < CHUNKS and len(group) == STEP_UNITS and all(arrival[i] <= now for i in needs):
+            chunks.append(ops)
+            ops = []
+            now += SOFTMAX
+            done += 1
+            continue
+        if done == CHUNKS and not pending:
+            break
+        later = [arrival[i] for i in arrival if arrival[i] > now]
+        if pending and due.get(pending[0], 1e9) > now:
+            later.append(due[pending[0]])
+        later += [free[w] - AHEAD_TIME + 0.001 for w, q in queues.items() if q and free[w] - AHEAD_TIME > now - 0.001]
+        if not later:
+            break
+        now = max(min(later), now + 1e-6)
+    chunks.append(ops)
     return order, chunks
 
 
 ORDER, PLAN = plan()
 UNIT_AT = {block: place for place, block in enumerate(ORDER)}
-
-
-def schedule():
-    held_at = {b: k for k, (waits, _) in enumerate(PLAN) for b in waits}
-    ahead = [([], []) for _ in range(CHUNKS + 1)]
-    k = 0
-    for c in range(CHUNKS):
-        step = c // 2
-        need = max(held_at[b] for b in ORDER[step * STEP_UNITS : (step + 1) * STEP_UNITS])
-        last = max(need, c)
-        while k <= last and k < len(PLAN):
-            ahead[c][0].append(k)
-            k += 1
-    while k < len(PLAN):
-        ahead[CHUNKS][0].append(k)
-        k += 1
-    return [a[0] for a in ahead]
-
-
-AHEAD = schedule()
+BOUNDS = [sum(PART_SIZES[:p]) for p in range(len(PART_SIZES) + 1)]
 
 
 def kernel(
@@ -156,33 +206,45 @@
         )
 
     send_place = {}
-    for _, starts in PLAN:
-        for b, way, target in starts:
-            send_place[(b, way)] = len(send_place)
-
-    def block_copy(b, way, target):
+    for ops in PLAN:
+        for op in ops:
+            if op[0] == "start":
+                send_place[op[1:3]] = len(send_place)
+
+    def slot(item, partner):
+        return 2 * UNIT_AT[item[1:]] + partner
+
+    def part_of(item, partner):
+        return buf.at[slot(item, partner), BOUNDS[item[0]] : BOUNDS[item[0] + 1]]
+
+    def landed(item, partner):
+        return recv_sem.at[item[0] * 2 * UNITS + slot(item, partner)]
+
+    def block_copy(item, way, target):
         axis, s = way
         device = at(y=s) if axis == "y" else at(z=s)
         return remote(
-            buf.at[2 * UNIT_AT[b]], buf.at[2 * UNIT_AT[target]],
-            send_sem.at[send_place[(b, way)]], recv_sem.at[2 * UNIT_AT[target]], device,
+            part_of(item, 0), part_of(target, 0), send_sem.at[send_place[(item, way)]], landed(target, 0), device
         )
 
-    def partner_copy(b):
-        u = UNIT_AT[b]
-        return remote(buf.at[2 * u], buf.at[2 * u + 1], part_sem.at[u], recv_sem.at[2 * u + 1], at(c=1))
-
-    def arrived(place):
-        return remote(buf.at[place], buf.at[place], part_sem.at[0], recv_sem.at[place], at(c=1))
-
-    def communicate(k):
-        waits, starts = PLAN[k]
-        for b in waits:
-            if b != (0, 0):
-                arrived(2 * UNIT_AT[b]).wait_recv()
-            partner_copy(b).start()
-        for b, way, target in starts:
-            block_copy(b, way, target).start()
+    def partner_copy(item):
+        sem = part_sem.at[item[0] * UNITS + UNIT_AT[item[1:]]]
+        return remote(part_of(item, 0), part_of(item, 1), sem, landed(item, 1), at(c=1))
+
+    def arrived(item, partner):
+        return remote(part_of(item, partner), part_of(item, partner), part_sem.at[0], landed(item, partner), at(c=1))
+
+    def perform(ops):
+        for op in ops:
+            if op[0] == "take":
+                if op[1][1:] != (0, 0):
+                    arrived(op[1], 0).wait_recv()
+            elif op[0] == "start":
+                block_copy(*op[1:]).start()
+            elif op[0] == "partner":
+                partner_copy(op[1]).start()
+            else:
+                tasks[op[1]]()
 
     x = decay_ref[...]
     lane = lax.broadcasted_iota(jnp.int32, (HEADS, TOK), 1)
@@ -237,7 +299,7 @@
         dec[h] = jnp.broadcast_to(d, (8, HD))
         return carry
 
-    lax.fori_loop(0, HEADS, local_state, 0)
+    lax.fori_loop(0, HEADS, local_state, 0, unroll=True)
 
     def to_partner(r, carry):
         h = other * HALF + r
@@ -245,13 +307,14 @@
         s_out[r, HD : HD + 16] = pack_decay(dec[h][0:1])
         return carry
 
-    lax.fori_loop(0, HALF, to_partner, 0)
+    lax.fori_loop(0, HALF, to_partner, 0, unroll=True)
     pl.semaphore_wait(barrier, len(peers))
     state_copy = remote(s_out, s_in, small_send.at[0], small_recv.at[0], at(c=1))
     state_copy.start()
     for load in kv_loads:
         load.wait()
-    communicate(0)
+    opening = next(n for n, op in enumerate(PLAN[0]) if op[0] == "task")
+    perform(PLAN[0][:opening])
 
     loads[3].wait()
     unit = jnp.where(row_i == col_i, 1.0, 0.0).astype(BF)
@@ -313,7 +376,7 @@
             qx[:, cols] = (qb.astype(F32) * jnp.exp(cb)).astype(BF)
             return carry
 
-        lax.fori_loop(0, HEADS, one, 0)
+        lax.fori_loop(0, HEADS, one, 0, unroll=True)
 
     def z_copy(d):
         head = lax.rem(me_z + d, NZ)
@@ -335,7 +398,7 @@
             z_out[r, HD : HD + 16] = pack_decay(d_mine * d_theirs)
             return carry
 
-        lax.fori_loop(0, HALF, one, 0)
+        lax.fori_loop(0, HALF, one, 0, unroll=True)
         for d in range(1, NZ):
             z_copy(d).start()
 
@@ -402,7 +465,7 @@
             c_out[r] = jnp.where(first, after, before).astype(BF)
             return carry
 
-        lax.fori_loop(0, HALF, one, 0)
+        lax.fori_loop(0, HALF, one, 0, unroll=True)
         remote(c_out, carr_b, small_send.at[24], small_recv.at[24], at(c=1)).start()
 
     def x_copy(d):
@@ -421,9 +484,11 @@
 
             return one
 
-        total = lax.fori_loop(0, HALF, half(carr_a, me_c * HALF), jnp.zeros((TOK, HD), F32))
+        total = lax.fori_loop(
+            0, HALF, half(carr_a, me_c * HALF), jnp.zeros((TOK, HD), F32), unroll=True
+        )
         remote(c_out, carr_b, small_send.at[24], small_recv.at[24], at(c=1)).wait_recv()
-        total = lax.fori_loop(0, HALF, half(carr_b, other * HALF), total)
+        total = lax.fori_loop(0, HALF, half(carr_b, other * HALF), total, unroll=True)
         x_out[...] = total
         for d in range(1, 4):
             x_copy(d).start()
@@ -444,30 +509,28 @@
             mixed_ref[:, cols] = (lin[:, cols] * inv * gain_ref[:, cols] * gated).astype(BF)
             return carry
 
-        lax.fori_loop(0, HEADS, one, 0)
-
-    TASKS = {0: intra, 1: chip_totals, 4: row_scan, 7: prefixes, 10: carries, 12: inter, 14: finish}
+        lax.fori_loop(0, HEADS, one, 0, unroll=True)
+
+    tasks = {
+        task.__name__: task for task in (intra, chip_totals, row_scan, prefixes, carries, inter, finish)
+    }
 
     def chunk(i, carry):
         for c in range(CHUNKS):
 
             @pl.when(i == c)
             def _(c=c):
-                for k in AHEAD[c]:
-                    if k > 0:
-                        communicate(k)
+                perform(PLAN[c][opening:] if c == 0 else PLAN[c])
                 if c % 2 == 0:
                     for u in range(c // 2 * STEP_UNITS, (c // 2 + 1) * STEP_UNITS):
-                        arrived(2 * u + 1).wait_recv()
-                if c in TASKS:
-                    TASKS[c]()
+                        for part in range(len(PART_SIZES)):
+                            arrived((part,) + ORDER[u], 1).wait_recv()
 
         softmax(i)
         return carry
 
     lax.fori_loop(0, CHUNKS, chunk, 0)
-    for k in AHEAD[CHUNKS]:
-        communicate(k)
+    perform(PLAN[CHUNKS])
 
     def result(h, carry):
         rows = pl.ds(pl.multiple_of(h * TOK, TOK), TOK)
@@ -486,18 +549,19 @@
     remote(c_out, carr_b, small_send.at[24], small_recv.at[24], at(c=1)).wait_send()
     for d in range(1, 4):
         x_copy(d).wait_send()
-    for waits, starts in PLAN:
-        for b in waits:
-            partner_copy(b).wait_send()
-        for b, way, target in starts:
-            block_copy(b, way, target).wait_send()
+    for ops in PLAN:
+        for op in ops:
+            if op[0] == "start":
+                block_copy(*op[1:]).wait_send()
+            elif op[0] == "partner":
+                partner_copy(op[1]).wait_send()
 
 
 def body(q_lin, k_lin, v_lin, log_decay, gate, norm_gain, queries, keys, values, order):
     vmem = pl.BlockSpec(memory_space=pltpu.VMEM)
     hbm = pl.BlockSpec(memory_space=pl.ANY)
     out = jax.ShapeDtypeStruct((TOK, WIDTH), BF)
-    n_sends = sum(len(starts) for _, starts in PLAN)
+    n_sends = sum(op[0] == "start" for ops in PLAN for op in ops)
     wide = pltpu.VMEM((TOK, WIDTH), BF)
     return pl.pallas_call(
         kernel,
@@ -533,9 +597,9 @@
             pltpu.SMEM((2 * UNITS,), jnp.int32),
             pltpu.SemaphoreType.DMA((5,)),
             pltpu.SemaphoreType.DMA((4,)),
-            pltpu.SemaphoreType.DMA((2 * UNITS,)),
+            pltpu.SemaphoreType.DMA((len(PART_SIZES) * 2 * UNITS,)),
             pltpu.SemaphoreType.DMA((n_sends,)),
-            pltpu.SemaphoreType.DMA((UNITS,)),
+            pltpu.SemaphoreType.DMA((len(PART_SIZES) * UNITS,)),
             pltpu.SemaphoreType.DMA((28,)),
             pltpu.SemaphoreType.DMA((28,)),
         ],

time: 87.3 us -> 69.8 us (0.80)
  Pallas kernels: 83.1 us -> 65.6 us
    pallas_call x1, Pallas kernels: 83.1 us -> 65.6 us  [body(): pl.pallas_call(kernel, out_shape=(out, out), in_specs=[hbm] * 7 + [vmem,...]
where the time goes in v2:
time: 69.8 us; the launch traced here: 69.7 us
  Pallas kernels  65.6 us (94%)
  local copies, waits for them, and re-layouts  2.74 us (4%)
  between operations  1.3 us (2%)
    pallas_call x1, Pallas kernels, body(): pl.pallas_call(kernel, out_shape=(out, out), in_specs=[hbm] * 7 + [vmem,...  65.6 us
    unnamed x4, local copies, waits for them, and re-layouts  2.74 us

profile of v2, /device:TPU:1, one launch (start us, length us, event | category | flops | bytes accessed | tf_op | source)
XLA Modules:
  0.0 69.7 jit_solution(1596158473419800957)
XLA Ops:
  1.3 65.6 %shard_map.113 = (bf16[128,2048]{1,0:T(8,128)(2,1)}, bf16[128,2048]{1,0:T(8,128)(2,1)}) custom-call(bf16[128,2048]{1,0:T(8,128)(2,1)} %q_hbm.1, bf16[128,2048]{1,0:T(8,128)(2,1)} %k_hbm.1, bf16[128,2048]{1,0:T(8,128)(2,1)} %v_hbm.1, bf16[128,2048]{1,0:T(8,128)(2,1)} %gate_hbm.1, bf16[128,2048]{1,0:T(8,128)(2,1)} %queries_hbm.1, bf16[128,256]{1,0:T(8,128)(2,1)} %keys_hbm.1, ...), custom_call_target="tpu_custom_call" | custom-call | tf_op jit(solution)/shard_map/pallas_call | solution.py:566
  66.9 0.0 copy-start
  66.9 1.9 %copy.15 = bf16[128,2048]{1,0:T(8,128)(2,1)} copy(bf16[128,2048]{1,0:T(8,128)(2,1)} %get-tuple-element.4) | data formatting | bytes 1048576
  68.9 0.0 copy-done
  68.9 0.8 %copy.16 = bf16[128,2048]{1,0:T(8,128)(2,1)} copy(bf16[128,2048]{1,0:T(8,128)(2,1)S(1)} %copy-done) | data formatting | bytes 1048576
Async XLA Ops:
  66.9 2.0 %copy-start = (bf16[128,2048]{1,0:T(8,128)(2,1)S(1)}, bf16[128,2048]{1,0:T(8,128)(2,1)}, u32[]{:S(2)}) copy-start(bf16[128,2048]{1,0:T(8,128)(2,1)} %get-tuple-element.5) | copy-start | bytes 1572868

commit v3 on v2

--- a/solution.py
+++ b/solution.py
@@ -23,11 +23,11 @@
 F32 = jnp.float32
 NY, NZ = 4, 8
 UNITS = NY * NZ
-STEP_UNITS = 4
+STEP_UNITS = 2
 SHARDS = 2 * STEP_UNITS
 KEYS = SHARDS * TOK
 STEPS = UNITS // STEP_UNITS
-CHUNKS = 2 * STEPS
+CHUNKS = STEPS
 
 
 def ring_next(r, size, tie_up):
@@ -47,7 +47,7 @@
 PART_SIZES = (4,)
 RATE, LATENCY = 104.0, 1.8
 CORE_RATE, CORE_LATENCY = 400.0, 1.1
-SOFTMAX, ISSUE, AHEAD_TIME = 1.9, 0.04, 2.0
+SOFTMAX, ISSUE, AHEAD_TIME = 1.85, 0.04, 2.0
 COST = {"intra": 2.0, "chip_totals": 0.7, "row_scan": 0.7, "prefixes": 0.4, "carries": 0.7, "inter": 1.2, "finish": 0.6}
 MESSAGES = {
     "chip_totals": [(("z", 1), 36 * 8), (("z", -1), 36 * 8)],
@@ -132,7 +132,7 @@
                 continue
             break
         issue()
-        group = order[done // 2 * STEP_UNITS : (done // 2 + 1) * STEP_UNITS]
+        group = order[done * STEP_UNITS : (done + 1) * STEP_UNITS]
         needs = [(p,) + b + (1,) for b in group for p in parts]
         if done < CHUNKS and len(group) == STEP_UNITS and all(arrival[i] <= now for i in needs):
             chunks.append(ops)
@@ -327,7 +327,7 @@
         acc[rows, :] = jnp.zeros((TOK, 2 * HD), F32)
         return carry
 
-    lax.fori_loop(0, HEADS, spread, 0)
+    lax.fori_loop(0, HEADS, spread, 0, unroll=True)
     for u, (dy, dz) in enumerate(ORDER):
         chip = lax.rem(me_y + dy, NY) * NZ + lax.rem(me_z + dz, NZ)
         shard_of[2 * u] = 2 * chip + me_c
@@ -336,31 +336,33 @@
     above = jnp.where(row_i > col_i, NEG, 0.0)
 
     def softmax(i):
-        g = lax.rem(i, 2)
-        base = lax.div(i, 2) * SHARDS
+        base = i * SHARDS
         for s in range(SHARDS):
             rows = slice(s * TOK, (s + 1) * TOK)
             shard = shard_of[base + s]
-            kaug[rows, 0:HD] = buf[base + s, g]
-            vaug[rows, :] = buf[base + s, 2 + g]
             whole = jnp.where(shard > my_shard, NEG, 0.0)
             part = jnp.where(shard == my_shard, 1.0, 0.0)
-            kaug[rows, HD : 2 * HD] = (above * part + whole).astype(BF)
-        rows = pl.ds(pl.multiple_of(g * GROUP * TOK, GROUP * TOK), GROUP * TOK)
-        sc = lax.dot_general(
-            qaug[rows, :], kaug[...], (((1,), (1,)), ((), ())), preferred_element_type=F32
-        )
-        old = top[rows, :]
-        new = jnp.maximum(old, jnp.max(sc, axis=1, keepdims=True))
-        w = jnp.exp2(sc * SCALE2 - jnp.tile(new * SCALE2, (1, SHARDS)))
-        alpha = jnp.exp2((old - new) * SCALE2)
-        pv = jnp.dot(w.astype(BF), vaug[...], preferred_element_type=F32)
-        acc[rows, 0:HD] = acc[rows, 0:HD] * alpha + pv
-        den = w[:, 0:HD]
-        for s in range(1, SHARDS):
-            den = den + w[:, s * HD : (s + 1) * HD]
-        acc[rows, HD : 2 * HD] = acc[rows, HD : 2 * HD] * alpha + den
-        top[rows, :] = new
+            bias = (above * part + whole).astype(BF)
+            for g in range(2):
+                kaug[g, rows, 0:HD] = buf[base + s, g]
+                kaug[g, rows, HD : 2 * HD] = bias
+                vaug[g, rows, :] = buf[base + s, 2 + g]
+        for g in range(2):
+            rows = slice(g * GROUP * TOK, (g + 1) * GROUP * TOK)
+            sc = lax.dot_general(
+                qaug[rows, :], kaug[g], (((1,), (1,)), ((), ())), preferred_element_type=F32
+            )
+            old = top[rows, :]
+            new = jnp.maximum(old, jnp.max(sc, axis=1, keepdims=True))
+            w = jnp.exp2(sc * SCALE2 - jnp.tile(new * SCALE2, (1, SHARDS)))
+            alpha = jnp.exp2((old - new) * SCALE2)
+            pv = jnp.dot(w.astype(BF), vaug[g], preferred_element_type=F32)
+            acc[rows, 0:HD] = acc[rows, 0:HD] * alpha + pv
+            den = w[:, 0:HD]
+            for s in range(1, SHARDS):
+                den = den + w[:, s * HD : (s + 1) * HD]
+            acc[rows, HD : 2 * HD] = acc[rows, HD : 2 * HD] * alpha + den
+            top[rows, :] = new
 
     def intra():
         loads[2].wait()
@@ -521,10 +523,9 @@
             @pl.when(i == c)
             def _(c=c):
                 perform(PLAN[c][opening:] if c == 0 else PLAN[c])
-                if c % 2 == 0:
-                    for u in range(c // 2 * STEP_UNITS, (c // 2 + 1) * STEP_UNITS):
-                        for part in range(len(PART_SIZES)):
-                            arrived((part,) + ORDER[u], 1).wait_recv()
+                for u in range(c * STEP_UNITS, (c + 1) * STEP_UNITS):
+                    for part in range(len(PART_SIZES)):
+                        arrived((part,) + ORDER[u], 1).wait_recv()
 
         softmax(i)
         return carry
@@ -538,7 +539,7 @@
         attended_ref[:, columns(h)] = (acc[rows, 0:HD] / den).astype(BF)
         return carry
 
-    lax.fori_loop(0, HEADS, result, 0)
+    lax.fori_loop(0, HEADS, result, 0, unroll=True)
 
     state_copy.wait_send()
     for d in range(1, NZ):
@@ -557,13 +558,18 @@
                 partner_copy(op[1]).wait_send()
 
 
+def hand_over(a_ref, b_ref, a_out, b_out):
+    a_out[...] = a_ref[...]
+    b_out[...] = b_ref[...]
+
+
 def body(q_lin, k_lin, v_lin, log_decay, gate, norm_gain, queries, keys, values, order):
     vmem = pl.BlockSpec(memory_space=pltpu.VMEM)
     hbm = pl.BlockSpec(memory_space=pl.ANY)
     out = jax.ShapeDtypeStruct((TOK, WIDTH), BF)
     n_sends = sum(op[0] == "start" for ops in PLAN for op in ops)
     wide = pltpu.VMEM((TOK, WIDTH), BF)
-    return pl.pallas_call(
+    mixed, attended = pl.pallas_call(
         kernel,
         out_shape=(out, out),
         in_specs=[hbm] * 7 + [vmem, vmem, pl.BlockSpec(memory_space=pltpu.SMEM)],
@@ -572,8 +578,8 @@
             wide, wide, wide, wide, wide,
             pltpu.VMEM((2 * UNITS, 4, TOK, HD), BF),
             pltpu.VMEM((HEADS * TOK, 2 * HD), BF),
-            pltpu.VMEM((KEYS, 2 * HD), BF),
-            pltpu.VMEM((KEYS, HD), BF),
+            pltpu.VMEM((2, KEYS, 2 * HD), BF),
+            pltpu.VMEM((2, KEYS, HD), BF),
             pltpu.VMEM((HEADS * TOK, HD), F32),
             pltpu.VMEM((HEADS * TOK, 2 * HD), F32),
             pltpu.VMEM((HEADS, TOK), F32),
@@ -609,6 +615,10 @@
     )(
         q_lin, k_lin, v_lin, gate, queries, keys, values, log_decay, norm_gain.reshape(1, WIDTH), order
     )
+    block = pl.BlockSpec((TOK // 4, WIDTH), lambda i: (i, 0))
+    return pl.pallas_call(
+        hand_over, grid=(4,), out_shape=(out, out), in_specs=[block, block], out_specs=(block, block)
+    )(mixed, attended)
 
 
 def solution(mesh):

time: 69.8 us -> 65.2 us (0.934)
  local copies, waits for them, and re-layouts: 2.74 us -> 0 us
  Pallas kernels: 65.6 us -> 63.7 us
    pallas_call x1, Pallas kernels: 65.6 us -> 60.3 us  [body(): pl.pallas_call(kernel, out_shape=(out, out), in_specs=[hbm] * 7 + [vmem,...]
    pallas_call x0 -> x1, Pallas kernels: none -> 3.41 us  [body(): pl.pallas_call(hand_over, grid=(4,), out_shape=(out, out), in_specs=[bloc...]
    unnamed x4 -> x0, local copies, waits for them, and re-layouts: 2.74 us -> none
where the time goes in v3:
time: 65.2 us; the launch traced here: 65 us
  Pallas kernels  63.7 us (98%)
  between operations  1.29 us (2%)
    pallas_call x1, Pallas kernels, body(): pl.pallas_call(kernel, out_shape=(out, out), in_specs=[hbm] * 7 + [vmem,...  60.3 us
    pallas_call x1, Pallas kernels, body(): pl.pallas_call(hand_over, grid=(4,), out_shape=(out, out), in_specs=[bloc...  3.41 us

profile of v3, /device:TPU:1, one launch (start us, length us, event | category | flops | bytes accessed | tf_op | source)
XLA Modules:
  0.0 65.0 jit_solution(5819263312940743442)
XLA Ops:
  1.3 60.3 %shard_map.113 = (bf16[128,2048]{1,0:T(8,128)(2,1)}, bf16[128,2048]{1,0:T(8,128)(2,1)}) custom-call(bf16[128,2048]{1,0:T(8,128)(2,1)} %q_hbm.1, bf16[128,2048]{1,0:T(8,128)(2,1)} %k_hbm.1, bf16[128,2048]{1,0:T(8,128)(2,1)} %v_hbm.1, bf16[128,2048]{1,0:T(8,128)(2,1)} %gate_hbm.1, bf16[128,2048]{1,0:T(8,128)(2,1)} %queries_hbm.1, bf16[128,256]{1,0:T(8,128)(2,1)} %keys_hbm.1, ...), custom_call_target="tpu_custom_call" | custom-call | tf_op jit(solution)/shard_map/pallas_call | solution.py:572
  61.6 3.4 %shard_map.114 = (bf16[128,2048]{1,0:T(8,128)(2,1)}, bf16[128,2048]{1,0:T(8,128)(2,1)}) custom-call(bf16[128,2048]{1,0:T(8,128)(2,1)} %get-tuple-element.4.a_ref, bf16[128,2048]{1,0:T(8,128)(2,1)} %get-tuple-element.5.b_ref), custom_call_target="tpu_custom_call" | custom-call | tf_op jit(solution)/shard_map/pallas_call | solution.py:619

commit v4 on v3

--- a/solution.py
+++ b/solution.py
@@ -308,6 +308,25 @@
         return carry
 
     lax.fori_loop(0, HALF, to_partner, 0, unroll=True)
+    loads[3].wait()
+    unit = jnp.where(row_i == col_i, 1.0, 0.0).astype(BF)
+
+    def spread(h, carry):
+        rows = pl.ds(pl.multiple_of(h * TOK, TOK), TOK)
+        qaug[rows, 0:HD] = qs[:, columns(h)]
+        qaug[rows, HD : 2 * HD] = unit
+        top[rows, :] = jnp.full((TOK, HD), NEG, F32)
+        acc[rows, :] = jnp.zeros((TOK, 2 * HD), F32)
+        return carry
+
+    lax.fori_loop(0, HEADS, spread, 0, unroll=True)
+    for u, (dy, dz) in enumerate(ORDER):
+        chip = lax.rem(me_y + dy, NY) * NZ + lax.rem(me_z + dz, NZ)
+        shard_of[2 * u] = 2 * chip + me_c
+        shard_of[2 * u + 1] = 2 * chip + other
+    my_shard = order_ref[0]
+    above = jnp.where(row_i > col_i, NEG, 0.0)
+
     pl.semaphore_wait(barrier, len(peers))
     state_copy = remote(s_out, s_in, small_send.at[0], small_recv.at[0], at(c=1))
     state_copy.start()
@@ -315,25 +334,6 @@
         load.wait()
     opening = next(n for n, op in enumerate(PLAN[0]) if op[0] == "task")
     perform(PLAN[0][:opening])
-
-    loads[3].wait()
-    unit = jnp.where(row_i == col_i, 1.0, 0.0).astype(BF)
-
-    def spread(h, carry):
-        rows = pl.ds(pl.multiple_of(h * TOK, TOK), TOK)
-        qaug[rows, 0:HD] = qs[:, columns(h)]
-        qaug[rows, HD : 2 * HD] = unit
-        top[rows, :] = jnp.full((TOK, HD), NEG, F32)
-        acc[rows, :] = jnp.zeros((TOK, 2 * HD), F32)
-        return carry
-
-    lax.fori_loop(0, HEADS, spread, 0, unroll=True)
-    for u, (dy, dz) in enumerate(ORDER):
-        chip = lax.rem(me_y + dy, NY) * NZ + lax.rem(me_z + dz, NZ)
-        shard_of[2 * u] = 2 * chip + me_c
-        shard_of[2 * u + 1] = 2 * chip + other
-    my_shard = order_ref[0]
-    above = jnp.where(row_i > col_i, NEG, 0.0)
 
     def softmax(i):
         base = i * SHARDS
@@ -558,9 +558,24 @@
                 partner_copy(op[1]).wait_send()
 
 
-def hand_over(a_ref, b_ref, a_out, b_out):
-    a_out[...] = a_ref[...]
-    b_out[...] = b_ref[...]
+def hand_over(a_ref, b_ref, a_out, b_out, held, in_sem, out_sem):
+    pieces = [(n, r) for n in range(2) for r in range(2)]
+    rows = [slice(r * TOK // 2, (r + 1) * TOK // 2) for r in range(2)]
+    loads = [
+        pltpu.make_async_copy((a_ref, b_ref)[n].at[rows[r]], held.at[n, rows[r]], in_sem.at[2 * n + r])
+        for n, r in pieces
+    ]
+    stores = [
+        pltpu.make_async_copy(held.at[n, rows[r]], (a_out, b_out)[n].at[rows[r]], out_sem.at[2 * n + r])
+        for n, r in pieces
+    ]
+    for load in loads:
+        load.start()
+    for load, store in zip(loads, stores):
+        load.wait()
+        store.start()
+    for store in stores:
+        store.wait()
 
 
 def body(q_lin, k_lin, v_lin, log_decay, gate, norm_gain, queries, keys, values, order):
@@ -615,9 +630,15 @@
     )(
         q_lin, k_lin, v_lin, gate, queries, keys, values, log_decay, norm_gain.reshape(1, WIDTH), order
     )
-    block = pl.BlockSpec((TOK // 4, WIDTH), lambda i: (i, 0))
     return pl.pallas_call(
-        hand_over, grid=(4,), out_shape=(out, out), in_specs=[block, block], out_specs=(block, block)
+        hand_over,
+        out_shape=(out, out),
+        in_specs=[hbm, hbm],
+        out_specs=(hbm, hbm),
+        scratch_shapes=[
+            pltpu.VMEM((2, TOK, WIDTH), BF), pltpu.SemaphoreType.DMA((4,)), pltpu.SemaphoreType.DMA((4,))
+        ],
+        compiler_params=pltpu.CompilerParams(vmem_limit_bytes=4 * 2**20),
     )(mixed, attended)
 
 

time: 65.2 us -> 64.7 us (level)
  Pallas kernels: 63.7 us -> 61.1 us
  local copies, waits for them, and re-layouts: 0 us -> 2.08 us
    pallas_call x1, Pallas kernels: 3.41 us -> 1.1 us  [body(): pl.pallas_call(hand_over, out_shape=(out, out), in_specs=[hbm, hbm], out_...]
    unnamed x0 -> x4, local copies, waits for them, and re-layouts: none -> 2.08 us
where the time goes in v4:
time: 64.7 us; the launch traced here: 64.5 us
  Pallas kernels  61.1 us (94%)
  local copies, waits for them, and re-layouts  2.08 us (3%)
  between operations  1.3 us (2%)
    pallas_call x1, Pallas kernels, body(): pl.pallas_call(kernel, out_shape=(out, out), in_specs=[hbm] * 7 + [vmem,...  60 us
    unnamed x4, local copies, waits for them, and re-layouts  2.08 us

profile of v4, /device:TPU:1, one launch (start us, length us, event | category | flops | bytes accessed | tf_op | source)
XLA Modules:
  0.0 64.5 jit_solution(3356858293213644477)
XLA Ops:
  1.3 60.0 %shard_map.113 = (bf16[128,2048]{1,0:T(8,128)(2,1)}, bf16[128,2048]{1,0:T(8,128)(2,1)}) custom-call(bf16[128,2048]{1,0:T(8,128)(2,1)} %q_hbm.1, bf16[128,2048]{1,0:T(8,128)(2,1)} %k_hbm.1, bf16[128,2048]{1,0:T(8,128)(2,1)} %v_hbm.1, bf16[128,2048]{1,0:T(8,128)(2,1)} %gate_hbm.1, bf16[128,2048]{1,0:T(8,128)(2,1)} %queries_hbm.1, bf16[128,256]{1,0:T(8,128)(2,1)} %keys_hbm.1, ...), custom_call_target="tpu_custom_call" | custom-call | tf_op jit(solution)/shard_map/pallas_call | solution.py:587
  61.3 0.0 copy-start
  61.3 1.0 %copy-done = bf16[128,2048]{1,0:T(8,128)(2,1)S(1)} copy-done((bf16[128,2048]{1,0:T(8,128)(2,1)S(1)}, bf16[128,2048]{1,0:T(8,128)(2,1)}, u32[]{:S(2)}) %copy-start) | copy-done | bytes 524312
  62.4 0.0 copy-start.1
  62.4 1.0 %copy-done.1 = bf16[128,2048]{1,0:T(8,128)(2,1)S(1)} copy-done((bf16[128,2048]{1,0:T(8,128)(2,1)S(1)}, bf16[128,2048]{1,0:T(8,128)(2,1)}, u32[]{:S(2)}) %copy-start.1) | copy-done | bytes 524312
  63.4 1.1 %shard_map.114 = (bf16[128,2048]{1,0:T(8,128)(2,1)}, bf16[128,2048]{1,0:T(8,128)(2,1)}) custom-call(bf16[128,2048]{1,0:T(8,128)(2,1)S(1)} %copy-done, bf16[128,2048]{1,0:T(8,128)(2,1)S(1)} %copy-done.1), custom_call_target="tpu_custom_call" | custom-call | tf_op jit(solution)/shard_map/pallas_call | solution.py:633
Async XLA Ops:
  61.3 1.0 %copy-start = (bf16[128,2048]{1,0:T(8,128)(2,1)S(1)}, bf16[128,2048]{1,0:T(8,128)(2,1)}, u32[]{:S(2)}) copy-start(bf16[128,2048]{1,0:T(8,128)(2,1)} %get-tuple-element.4.a_ref) | copy-start | bytes 1572868
  62.4 1.0 %copy-start.1 = (bf16[128,2048]{1,0:T(8,128)(2,1)S(1)}, bf16[128,2048]{1,0:T(8,128)(2,1)}, u32[]{:S(2)}) copy-start(bf16[128,2048]{1,0:T(8,128)(2,1)} %get-tuple-element.5.b_ref) | copy-start | bytes 1572868
